TPU v7x, 256 devices: a whole 4x4x8 slice. The times are simulated.
256 devices in a mesh: section: 16 (over z_lo, y), dp: 16 (over x, z_hi, core).
Axes of the slice: x: 4, y: 4, z: 8 (z_hi: 2, z_lo: 4; z = z_hi * 4 + z_lo), core: 2. Of those that a mesh axis runs over, the one named last changes fastest.
Arguments:
- enc_state: bfloat16 [16, 512, 4096], P('section', 'dp'), may hold values from -1000 to 1000
- final_gain: float32 [4096], replicated, may hold values from 0.5 to 1.5
- queries: bfloat16 [16, 2048, 4096], P('section', 'dp'), may hold values from -60 to 60
- w_key: bfloat16 [16, 4096, 4096], P('section', None, 'dp'), may hold values from -0.09375 to 0.09375
- w_value: bfloat16 [16, 4096, 4096], P('section', None, 'dp'), may hold values from -0.09375 to 0.09375
- ctx_grad: bfloat16 [16, 2048, 4096], P('section', 'dp'), may hold values from -6 to 6
- mem_len: int32 [16], P('dp'), may hold values from 8 to 32, as said below
Outputs:
- query_grad: bfloat16 [16, 2048, 4096], P('section', 'dp')
- key_weight_grad: bfloat16 [16, 4096, 4096], P('section', None, 'dp')
- value_weight_grad: bfloat16 [16, 4096, 4096], P('section', None, 'dp')
- state_grad: bfloat16 [16, 512, 4096], P('section', 'dp')
- gain_grad: float32 [4096], replicated
Inputs may be any that keep to these rules, and one draw needn't show every extreme that they name: Sequence b's memory holds mem_len[b] valid tokens from position 0; in every draw some sequence has all 32.
All inputs are finite; a program needn't handle non-finite values.
Results may differ from a plain program's by a relative error of at most 0.028.
The roundings to bfloat16 on the way count: a program that leaves them out, or rounds other values in their place, can miss the bound.
Values may be sent and summed in bfloat16 or wider, within the bound.
A program may use at most 64 MiB of HBM per device.

v0:
```python
import jax
import jax.numpy as jnp
from jax import lax
from jax.sharding import PartitionSpec as P

HEAD_DIM = 256
epsilon = 1e-06


def broadcast(block, axis, holder):
    block = jnp.where(lax.axis_index(axis) == holder, block, jnp.zeros_like(block))
    return lax.psum(block, axis)


def on_device(enc_state, final_gain, queries, w_key, w_value, ctx_grad, mem_len):
    sections = lax.axis_size("section")
    replicas = lax.axis_size("dp")
    section_index = lax.axis_index("section")
    last_encoder = sections // 2 - 1
    is_decoder = (section_index > last_encoder).astype(jnp.float32)
    is_last = (section_index == last_encoder).astype(jnp.float32)
    src_len = enc_state.shape[1]
    tgt_len = queries.shape[1]
    local_width = w_key.shape[2]
    heads_here = local_width // HEAD_DIM
    score_scale = HEAD_DIM ** (-0.5)
    enc_rows = enc_state[0].astype(jnp.float32)
    inverse = lax.rsqrt(jnp.mean(enc_rows * enc_rows, axis=1, keepdims=True) + epsilon)
    normed = enc_rows * inverse
    memory = (normed * final_gain).astype(jnp.bfloat16)
    sent = broadcast(memory, "section", last_encoder)
    all_memory, all_len = (
        lax.all_gather(sent, "dp", axis=0, tiled=True),
        lax.all_gather(mem_len, "dp", axis=0, tiled=True),
    )
    w_both = jnp.concatenate([w_key[0], w_value[0]], axis=1)
    projected = jnp.dot(all_memory, w_both, preferred_element_type=jnp.float32).astype(jnp.bfloat16)
    key_rows = projected[:, :local_width].reshape(replicas, src_len, heads_here, HEAD_DIM)
    value_rows = projected[:, local_width:].reshape(replicas, src_len, heads_here, HEAD_DIM)
    query_heads, grad_heads = (
        lax.all_to_all(queries[0], "dp", split_axis=1, concat_axis=0, tiled=True),
        lax.all_to_all(ctx_grad[0], "dp", split_axis=1, concat_axis=0, tiled=True),
    )
    query_rows = query_heads.reshape(replicas, tgt_len, heads_here, HEAD_DIM)
    grad_rows = grad_heads.reshape(replicas, tgt_len, heads_here, HEAD_DIM)
    key_valid = jnp.arange(src_len, dtype=jnp.int32)[None, :] < all_len[:, None]
    scores = (
        jnp.einsum("btha,buha->bhut", query_rows, key_rows, preferred_element_type=jnp.float32)
        * score_scale
    )
    scores = jnp.where(key_valid[:, None, :, None], scores, -1e30)
    row_max = jnp.max(scores, axis=2, keepdims=True)
    exponent = jnp.exp(scores - row_max)
    probs = exponent / jnp.sum(exponent, axis=2, keepdims=True)
    probs_low = probs.astype(jnp.bfloat16)
    grad_probs = jnp.einsum(
        "btha,buha->bhut", grad_rows, value_rows, preferred_element_type=jnp.float32
    )
    row_delta = jnp.sum(probs * grad_probs, axis=2, keepdims=True)
    grad_scores = (probs * (grad_probs - row_delta) * score_scale).astype(jnp.bfloat16)
    query_grad_heads = (
        jnp.einsum("bhut,buha->btha", grad_scores, key_rows, preferred_element_type=jnp.float32)
        .astype(jnp.bfloat16)
        .reshape(replicas * tgt_len, local_width)
    )
    key_grad = (
        jnp.einsum("bhut,btha->buha", grad_scores, query_rows, preferred_element_type=jnp.float32)
        .astype(jnp.bfloat16)
        .reshape(replicas * src_len, local_width)
    )
    value_grad = (
        jnp.einsum("bhut,btha->buha", probs_low, grad_rows, preferred_element_type=jnp.float32)
        .astype(jnp.bfloat16)
        .reshape(replicas * src_len, local_width)
    )
    both_grads = jnp.concatenate([key_grad, value_grad], axis=1)
    weight_grads = (
        lax.dot_general(
            all_memory, both_grads, (((0,), (0,)), ((), ())), preferred_element_type=jnp.float32
        )
        * is_decoder
    ).astype(jnp.bfloat16)
    query_back = lax.all_to_all(query_grad_heads, "dp", split_axis=0, concat_axis=1, tiled=True)
    query_grad = (query_back.astype(jnp.float32) * is_decoder).astype(jnp.bfloat16)[None]
    section_part = lax.psum_scatter(
        (
            lax.dot_general(
                both_grads, w_both, (((1,), (1,)), ((), ())), preferred_element_type=jnp.float32
            )
            * is_decoder
        ).astype(jnp.bfloat16),
        "dp",
        scatter_dimension=0,
        tiled=True,
    )
    memory_grad = lax.psum(section_part, "section").astype(jnp.float32)
    scaled_grad = memory_grad * final_gain
    last_grad = inverse * (
        scaled_grad - normed * jnp.mean(scaled_grad * normed, axis=1, keepdims=True)
    )
    state_grad = (last_grad * is_last).astype(jnp.bfloat16)[None]
    gain_grad = lax.psum(jnp.sum(memory_grad * normed, axis=0) * is_last, ("section", "dp"))
    key_weight_grad = weight_grads[:, :local_width][None]
    value_weight_grad = weight_grads[:, local_width:][None]
    return (query_grad, key_weight_grad, value_weight_grad, state_grad, gain_grad)


def solution(mesh):
    placed = (
        P("section", "dp", None),
        P(),
        P("section", "dp", None),
        P("section", None, "dp"),
        P("section", None, "dp"),
        P("section", "dp", None),
        P("dp"),
    )
    return jax.shard_map(
        on_device,
        mesh=mesh,
        in_specs=placed,
        out_specs=(
            P("section", "dp", None),
            P("section", None, "dp"),
            P("section", None, "dp"),
            P("section", "dp", None),
            P(),
        ),
        check_vma=False,
    )
```

profile of v0, /device:TPU:1, one launch (start us, length us, event | category | flops | bytes accessed | tf_op | source)
XLA Modules:
  0.0 639.9 jit_solution(12333519288310503521)
XLA Ops:
  7.2 1.2 fusion.28
  8.4 1.8 fusion.33
  10.3 156.1 %all-reduce.4.cloned.1.call-done = bf16[32,4096]{1,0:T(8,128)(2,1)} async-done(((bf16[32,4096]{1,0:T(8,128)(2,1)}), bf16[32,4096]{1,0:T(8,128)(2,1)}) %all-reduce.4.cloned.1.call-update) | async-done | bytes 262160 | tf_op jit(solution)/shard_map/psum | solution.py:12
  166.4 1.6 copy.13
  168.0 1.3 copy.14
  169.3 19.1 %all-to-all-start = ((bf16[128,16,256]{2,0,1:T(8,128)(2,1)}), bf16[128,16,256]{2,0,1:T(8,128)(2,1)S(1)}, u32[]{:S(2)}, u32[]{:S(2)}) async-start(bf16[128,16,256]{2,0,1:T(8,128)(2,1)} %copy.14), calls=%async_computation | async-start | bytes 2097152 | tf_op jit(solution)/shard_map/all_to_all | solution.py:41
  188.4 0.7 copy.15
  189.1 1.3 copy.16
  190.4 26.1 %all-to-all-done = bf16[128,16,256]{2,0,1:T(8,128)(2,1)S(1)} async-done(((bf16[128,16,256]{2,0,1:T(8,128)(2,1)}), bf16[128,16,256]{2,0,1:T(8,128)(2,1)S(1)}, u32[]{:S(2)}, u32[]{:S(2)}) %all-to-all-start) | async-done | bytes 1048608 | tf_op jit(solution)/shard_map/all_to_all | solution.py:41
  216.5 7.5 %all-to-all-start.1 = ((bf16[128,16,256]{2,0,1:T(8,128)(2,1)}), bf16[128,16,256]{2,0,1:T(8,128)(2,1)S(1)}, u32[]{:S(2)}, u32[]{:S(2)}) async-start(bf16[128,16,256]{2,0,1:T(8,128)(2,1)} %copy.16), calls=%async_computation.1 | async-start | bytes 2097152 | tf_op jit(solution)/shard_map/all_to_all | solution.py:42
  224.7 0.6 dynamic-slice
  225.3 0.8 dynamic-update-slice
  226.0 33.3 %all-reduce = s32[16]{0:T(128)S(1)} all-reduce(s32[16]{0:T(128)S(1)} %dynamic-update-slice), channel_id=1, replica_groups=mesh['section'=16,'dp'=16] {'dp'}, use_global_device_ids=true, to_apply=%add | all-reduce | flops 16 | bytes 128
  259.4 15.6 %all-gather.2.cloned.1.call-done = bf16[512,4096]{1,0:T(8,128)(2,1)} async-done(((bf16[32,4096]{1,0:T(8,128)(2,1)}), bf16[512,4096]{1,0:T(8,128)(2,1)}) %all-gather.2.cloned.1.call-update) | async-done | bytes 4194320 | tf_op jit(solution)/shard_map/all_gather | solution.py:33
  275.0 5.8 fusion.4
  280.8 0.5 fusion.10
  281.3 0.6 fusion.46
  281.9 0.5 fusion.13
  282.4 0.3 convolution_convert_fusion.1
  282.7 0.3 convolution_convert_fusion.2
  283.0 6.6 %multiply_convert_fusion = bf16[512,4096]{1,0:T(8,128)(2,1)} fusion(f32[]{:T(128)S(6)} %convert_element_type.108, bf16[4096,256]{1,0:T(8,128)(2,1)} %bitcast.67, bf16[4096,256]{1,0:T(8,128)(2,1)} %bitcast.69, bf16[512,256]{1,0:T(8,128)(2,1)S(1)} %bitcast.70, bf16[512,256]{1,0:T(8,128)(2,1)S(1)} %bitcast.72), kind=kOutput, calls=%fused_computation.2 | convolution fusion | flops 2161115136 | bytes 8912900 | tf_op jit(solution)/shard_map/dot_general | solution.py:87
  289.6 1.5 fusion.3
  291.1 3.7 all-to-all-start.2
  294.8 4.6 multiply_convert_fusion.1
  299.4 2.3 slice_bitcast_fusion
  301.7 91.4 %reduce-scatter.2.cloned.1.call-done = bf16[32,4096]{1,0:T(8,128)(2,1)} async-done(((bf16[512,4096]{1,0:T(8,128)(2,1)}), bf16[32,4096]{1,0:T(8,128)(2,1)}) %reduce-scatter.2.cloned.1.call-update) | async-done | bytes 262160 | tf_op jit(solution)/shard_map/reduce_scatter | solution.py:85
  393.2 0.3 multiply_convert_fusion.2
  393.5 1.3 copy.17
  394.8 150.1 %all-reduce.6.cloned.1.call-done = bf16[32,4096]{1,0:T(8,128)(2,1)} async-done(((bf16[32,4096]{1,0:T(8,128)(2,1)}), bf16[32,4096]{1,0:T(8,128)(2,1)}) %all-reduce.6.cloned.1.call-update) | async-done | bytes 262160 | tf_op jit(solution)/shard_map/psum | solution.py:96
  544.9 1.3 fusion.27
  546.2 85.3 %psum.23 = f32[4096]{0:T(1024)} all-reduce(f32[4096]{0:T(1024)S(1)} %broadcast_multiply_fusion), channel_id=1, replica_groups=mesh['section'=16,'dp'=16] {'section','dp'}, use_global_device_ids=true, to_apply=%region_9.10 | all-reduce | flops 4096 | bytes 32768 | tf_op jit(solution)/shard_map/psum | solution.py:102
  631.5 1.8 fusion.34
  (24 shorter events, 0.4 us)
Async XLA Ops:
  7.2 181.2 %copy-start.1 = (bf16[1,128,4096]{2,1,0:T(8,128)(2,1)S(1)}, bf16[1,128,4096]{2,1,0:T(8,128)(2,1)}, u32[]{:S(2)}) copy-start(bf16[1,128,4096]{2,1,0:T(8,128)(2,1)} %param.12) | copy-start | bytes 3145732
  7.2 159.2 %all-reduce.4.cloned.1.call-start = ((), (), s32[]{:S(2)}) async-start(), calls=%async_computation.4 | async-start | bytes 524288 | tf_op jit(solution)/shard_map/psum | solution.py:12
  10.3 264.7 %all-gather.2.cloned.1.call-start = ((), (), s32[]{:S(2)}) async-start(), calls=%async_computation.5 | async-start | bytes 4456448 | tf_op jit(solution)/shard_map/all_gather | solution.py:33
  169.3 55.3 %copy-start.3 = (u32[256]{0:T(256)S(1)}, u32[256]{0:T(256)}, u32[]{:S(2)}) copy-start(u32[256]{0:T(256)} %constant.31) | copy-start | bytes 3076
  169.3 47.2 %all-to-all-start = ((bf16[128,16,256]{2,0,1:T(8,128)(2,1)}), bf16[128,16,256]{2,0,1:T(8,128)(2,1)S(1)}, u32[]{:S(2)}, u32[]{:S(2)}) async-start(bf16[128,16,256]{2,0,1:T(8,128)(2,1)} %copy.14), calls=%async_computation | async-start | bytes 2097152 | tf_op jit(solution)/shard_map/all_to_all | solution.py:41
  216.5 65.4 %all-to-all-start.1 = ((bf16[128,16,256]{2,0,1:T(8,128)(2,1)}), bf16[128,16,256]{2,0,1:T(8,128)(2,1)S(1)}, u32[]{:S(2)}, u32[]{:S(2)}) async-start(bf16[128,16,256]{2,0,1:T(8,128)(2,1)} %copy.16), calls=%async_computation.1 | async-start | bytes 2097152 | tf_op jit(solution)/shard_map/all_to_all | solution.py:42
  224.0 169.2 %reduce-scatter.2.cloned.1.call-start = ((), (), s32[]{:S(2)}) async-start(), calls=%async_computation.6 | async-start | bytes 4456448 | tf_op jit(solution)/shard_map/reduce_scatter | solution.py:85
  291.1 102.1 %all-to-all-start.2 = ((bf16[16,128,256]{1,2,0:T(8,128)(2,1)}), bf16[16,128,256]{1,2,0:T(8,128)(2,1)S(1)}, u32[]{:S(2)}, u32[]{:S(2)}) async-start(bf16[16,128,256]{1,2,0:T(8,128)(2,1)} %fusion.3), calls=%async_computation.2 | async-start | bytes 2097152 | tf_op jit(solution)/shard_map/all_to_all | solution.py:83
  294.8 250.1 %all-reduce.6.cloned.1.call-start = ((), (), s32[]{:S(2)}) async-start(), calls=%async_computation.7 | async-start | bytes 524288 | tf_op jit(solution)/shard_map/psum | solution.py:96
  301.7 243.2 %copy-start = (bf16[1,32,4096]{2,1,0:T(8,128)(2,1)S(1)}, bf16[1,32,4096]{2,1,0:T(8,128)(2,1)}, u32[]{:S(2)}) copy-start(bf16[1,32,4096]{2,1,0:T(8,128)(2,1)} %param.7) | copy-start | bytes 786436
  301.7 243.2 %copy-start.2 = (f32[4096]{0:T(1024)S(1)}, f32[4096]{0:T(1024)}, u32[]{:S(2)}) copy-start(f32[4096]{0:T(1024)} %param.8) | copy-start | bytes 49156
Sparse Core Ops, SparseCore 0:
  11.2 155.1 all-reduce.3
  169.1 105.8 all-gather.1
  289.7 103.3 reduce-scatter.1
  395.6 149.2 all-reduce.5
where the time goes:
time: 640 us
  waiting for transfers between devices  439 us (69%)
  blocking collectives  119 us (19%)
  starting transfers between devices  30.4 us (5%)
  matrix products  19.9 us (3%)
  between operations  14.6 us (2%)
  local copies, waits for them, and re-layouts  9.89 us (2%)
  other arithmetic  7.1 us (1%)
    psum x1, waiting for transfers between devices, broadcast(): return lax.psum(block, axis)  156 us
    psum x1, waiting for transfers between devices, on_device(): memory_grad = lax.psum(section_part, 'section').astype(jnp.float32)  150 us
    reduce_scatter x1, waiting for transfers between devices, on_device(): lax.psum_scatter((lax.dot_general(both_grads, w_both, (((1,), (1,)), ((),...  91.4 us
    psum x1, blocking collectives, on_device(): lax.psum(jnp.sum(memory_grad * normed, axis=0) * is_last, ('section', 'dp'))  85.3 us
    unnamed x1, blocking collectives  33.3 us
    all_to_all x1, waiting for transfers between devices, on_device(): lax.all_to_all(queries[0], 'dp', split_axis=1, concat_axis=0, tiled=True)  26.1 us
    all_to_all x1, starting transfers between devices, on_device(): lax.all_to_all(queries[0], 'dp', split_axis=1, concat_axis=0, tiled=True)  19.1 us
    all_gather x1, waiting for transfers between devices, on_device(): lax.all_gather(sent, 'dp', axis=0, tiled=True)  15.6 us
  transfers between devices with their start and end apart: 7, of which 5 were waited for; matrix products, arithmetic and copies ran while one was open for 4% of the time, Pallas kernels for 0%

commit v1 on v0

--- a/solution.py
+++ b/solution.py
@@ -99,7 +99,7 @@
         scaled_grad - normed * jnp.mean(scaled_grad * normed, axis=1, keepdims=True)
     )
     state_grad = (last_grad * is_last).astype(jnp.bfloat16)[None]
-    gain_grad = lax.psum(jnp.sum(memory_grad * normed, axis=0) * is_last, ("section", "dp"))
+    gain_grad = lax.psum(lax.psum(jnp.sum(memory_grad * normed, axis=0) * is_last, "dp"), "section")
     key_weight_grad = weight_grads[:, :local_width][None]
     value_weight_grad = weight_grads[:, local_width:][None]
     return (query_grad, key_weight_grad, value_weight_grad, state_grad, gain_grad)

time: 640 us -> 726 us (1.13)
  the two profiles are of different devices: /device:TPU:1 before, /device:TPU:0 now
where the time goes in v1:
time: 726 us; the launch traced here: 725 us
  waiting for transfers between devices  457 us (63%)
  blocking collectives  198 us (27%)
  matrix products  20 us (3%)
  starting transfers between devices  19.2 us (3%)
  between operations  14.6 us (2%)
  local copies, waits for them, and re-layouts  9.89 us (1%)
    psum x1, waiting for transfers between devices, broadcast(): return lax.psum(block, axis)  164 us
    psum x1, waiting for transfers between devices, on_device(): memory_grad = lax.psum(section_part, 'section').astype(jnp.float32)  158 us
    reduce_scatter x1, waiting for transfers between devices, on_device(): lax.psum_scatter((lax.dot_general(both_grads, w_both, (((1,), (1,)), ((),...  94 us
    psum x1, blocking collectives, on_device(): lax.psum(jnp.sum(memory_grad * normed, axis=0) * is_last, 'dp')  84.2 us
    psum x1, blocking collectives, on_device(): lax.psum(lax.psum(jnp.sum(memory_grad * normed, axis=0) * is_last, 'dp'),...  79.1 us
    unnamed x1, blocking collectives  34.6 us
    all_to_all x1, waiting for transfers between devices, on_device(): lax.all_to_all(queries[0], 'dp', split_axis=1, concat_axis=0, tiled=True)  26.5 us
  transfers between devices with their start and end apart: 7, of which 5 were waited for; matrix products, arithmetic and copies ran while one was open for 3% of the time, Pallas kernels for 0%

profile of v1, /device:TPU:0, one launch (start us, length us, event | category | flops | bytes accessed | tf_op | source)
XLA Modules:
  0.0 725.5 jit_solution(6851115538229664736)
XLA Ops:
  7.2 1.2 fusion.28
  8.4 1.8 fusion.33
  10.3 163.6 %all-reduce.4.cloned.1.call-done = bf16[32,4096]{1,0:T(8,128)(2,1)} async-done(((bf16[32,4096]{1,0:T(8,128)(2,1)}), bf16[32,4096]{1,0:T(8,128)(2,1)}) %all-reduce.4.cloned.1.call-update) | async-done | bytes 262160 | tf_op jit(solution)/shard_map/psum | solution.py:12
  174.0 1.6 copy.13
  175.6 1.3 copy.14
  176.9 8.4 %all-to-all-start = ((bf16[128,16,256]{2,0,1:T(8,128)(2,1)}), bf16[128,16,256]{2,0,1:T(8,128)(2,1)S(1)}, u32[]{:S(2)}, u32[]{:S(2)}) async-start(bf16[128,16,256]{2,0,1:T(8,128)(2,1)} %copy.14), calls=%async_computation | async-start | bytes 2097152 | tf_op jit(solution)/shard_map/all_to_all | solution.py:41
  185.3 0.7 copy.15
  186.0 1.3 copy.16
  187.3 26.5 %all-to-all-done = bf16[128,16,256]{2,0,1:T(8,128)(2,1)S(1)} async-done(((bf16[128,16,256]{2,0,1:T(8,128)(2,1)}), bf16[128,16,256]{2,0,1:T(8,128)(2,1)S(1)}, u32[]{:S(2)}, u32[]{:S(2)}) %all-to-all-start) | async-done | bytes 1048608 | tf_op jit(solution)/shard_map/all_to_all | solution.py:41
  213.8 7.0 all-to-all-start.1
  221.6 0.6 dynamic-slice
  222.2 0.8 dynamic-update-slice
  222.9 34.6 %all-reduce = s32[16]{0:T(128)S(1)} all-reduce(s32[16]{0:T(128)S(1)} %dynamic-update-slice), channel_id=1, replica_groups=mesh['section'=16,'dp'=16] {'dp'}, use_global_device_ids=true, to_apply=%add | all-reduce | flops 16 | bytes 128
  257.6 14.4 %all-gather.2.cloned.1.call-done = bf16[512,4096]{1,0:T(8,128)(2,1)} async-done(((bf16[32,4096]{1,0:T(8,128)(2,1)}), bf16[512,4096]{1,0:T(8,128)(2,1)}) %all-gather.2.cloned.1.call-update) | async-done | bytes 4194320 | tf_op jit(solution)/shard_map/all_gather | solution.py:33
  272.1 5.8 fusion.4
  277.9 0.5 fusion.10
  278.4 0.6 fusion.46
  279.0 0.5 fusion.13
  279.5 0.3 convolution_convert_fusion.1
  279.8 0.3 convolution_convert_fusion.2
  280.1 6.6 multiply_convert_fusion
  286.7 1.5 fusion.3
  288.1 3.7 all-to-all-start.2
  291.9 4.6 multiply_convert_fusion.1
  296.4 2.3 slice_bitcast_fusion
  298.7 94.0 %reduce-scatter.2.cloned.1.call-done = bf16[32,4096]{1,0:T(8,128)(2,1)} async-done(((bf16[512,4096]{1,0:T(8,128)(2,1)}), bf16[32,4096]{1,0:T(8,128)(2,1)}) %reduce-scatter.2.cloned.1.call-update) | async-done | bytes 262160 | tf_op jit(solution)/shard_map/reduce_scatter | solution.py:85
  393.0 1.3 copy.17
  394.3 158.1 %all-reduce.6.cloned.1.call-done = bf16[32,4096]{1,0:T(8,128)(2,1)} async-done(((bf16[32,4096]{1,0:T(8,128)(2,1)}), bf16[32,4096]{1,0:T(8,128)(2,1)}) %all-reduce.6.cloned.1.call-update) | async-done | bytes 262160 | tf_op jit(solution)/shard_map/psum | solution.py:96
  552.5 1.3 fusion.27
  553.7 84.2 %psum.30 = f32[4096]{0:T(1024)S(1)} all-reduce(f32[4096]{0:T(1024)S(1)} %broadcast_multiply_fusion), channel_id=1, replica_groups=mesh['section'=16,'dp'=16] {'dp'}, use_global_device_ids=true, to_apply=%region_9.10 | all-reduce | flops 4096 | bytes 32768 | tf_op jit(solution)/shard_map/psum | solution.py:102
  637.9 79.1 %psum.31 = f32[4096]{0:T(1024)} all-reduce(f32[4096]{0:T(1024)S(1)} %psum.30), channel_id=1, replica_groups=mesh['section'=16,'dp'=16] {'section'}, use_global_device_ids=true, to_apply=%region_10.11 | all-reduce | flops 4096 | bytes 32768 | tf_op jit(solution)/shard_map/psum | solution.py:102
  717.1 1.8 fusion.34
  (25 shorter events, 0.7 us)
Async XLA Ops:
  7.2 178.1 %copy-start.1 = (bf16[1,128,4096]{2,1,0:T(8,128)(2,1)S(1)}, bf16[1,128,4096]{2,1,0:T(8,128)(2,1)}, u32[]{:S(2)}) copy-start(bf16[1,128,4096]{2,1,0:T(8,128)(2,1)} %param.12) | copy-start | bytes 3145732
  7.2 166.8 %all-reduce.4.cloned.1.call-start = ((), (), s32[]{:S(2)}) async-start(), calls=%async_computation.4 | async-start | bytes 524288 | tf_op jit(solution)/shard_map/psum | solution.py:12
  10.3 261.8 %all-gather.2.cloned.1.call-start = ((), (), s32[]{:S(2)}) async-start(), calls=%async_computation.5 | async-start | bytes 4456448 | tf_op jit(solution)/shard_map/all_gather | solution.py:33
  176.9 44.7 %copy-start.3 = (u32[256]{0:T(256)S(1)}, u32[256]{0:T(256)}, u32[]{:S(2)}) copy-start(u32[256]{0:T(256)} %constant.31) | copy-start | bytes 3076
  176.9 36.9 %all-to-all-start = ((bf16[128,16,256]{2,0,1:T(8,128)(2,1)}), bf16[128,16,256]{2,0,1:T(8,128)(2,1)S(1)}, u32[]{:S(2)}, u32[]{:S(2)}) async-start(bf16[128,16,256]{2,0,1:T(8,128)(2,1)} %copy.14), calls=%async_computation | async-start | bytes 2097152 | tf_op jit(solution)/shard_map/all_to_all | solution.py:41
  213.8 65.2 %all-to-all-start.1 = ((bf16[128,16,256]{2,0,1:T(8,128)(2,1)}), bf16[128,16,256]{2,0,1:T(8,128)(2,1)S(1)}, u32[]{:S(2)}, u32[]{:S(2)}) async-start(bf16[128,16,256]{2,0,1:T(8,128)(2,1)} %copy.16), calls=%async_computation.1 | async-start | bytes 2097152 | tf_op jit(solution)/shard_map/all_to_all | solution.py:42
  220.9 171.9 %reduce-scatter.2.cloned.1.call-start = ((), (), s32[]{:S(2)}) async-start(), calls=%async_computation.6 | async-start | bytes 4456448 | tf_op jit(solution)/shard_map/reduce_scatter | solution.py:85
  288.1 104.6 %all-to-all-start.2 = ((bf16[16,128,256]{1,2,0:T(8,128)(2,1)}), bf16[16,128,256]{1,2,0:T(8,128)(2,1)S(1)}, u32[]{:S(2)}, u32[]{:S(2)}) async-start(bf16[16,128,256]{1,2,0:T(8,128)(2,1)} %fusion.3), calls=%async_computation.2 | async-start | bytes 2097152 | tf_op jit(solution)/shard_map/all_to_all | solution.py:83
  291.8 260.6 %all-reduce.6.cloned.1.call-start = ((), (), s32[]{:S(2)}) async-start(), calls=%async_computation.7 | async-start | bytes 524288 | tf_op jit(solution)/shard_map/psum | solution.py:96
  298.7 253.7 %copy-start = (bf16[1,32,4096]{2,1,0:T(8,128)(2,1)S(1)}, bf16[1,32,4096]{2,1,0:T(8,128)(2,1)}, u32[]{:S(2)}) copy-start(bf16[1,32,4096]{2,1,0:T(8,128)(2,1)} %param.7) | copy-start | bytes 786436
  298.7 253.7 %copy-start.2 = (f32[4096]{0:T(1024)S(1)}, f32[4096]{0:T(1024)}, u32[]{:S(2)}) copy-start(f32[4096]{0:T(1024)} %param.8) | copy-start | bytes 49156
Sparse Core Ops, SparseCore 0:
  11.2 162.7 all-reduce.3
  176.6 95.3 all-gather.1
  286.8 105.8 reduce-scatter.1
  395.2 157.2 all-reduce.5
